TPU v7x, 128 devices: a whole 4x4x4 slice. The times are simulated.
128 devices in a mesh: dp: 8 (over z_lo, y), pipe: 16 (over z_hi, x, core).
Axes of the slice: x: 4, y: 4, z: 4 (z_hi: 2, z_lo: 2; z = z_hi * 2 + z_lo), core: 2. Of those that a mesh axis runs over, the one named last changes fastest.
Arguments:
- activations: bfloat16 [16, 4096, 8192], P('pipe', 'dp'), may hold values from -6 to 6
- cotangent: bfloat16 [4096, 8192], P('dp'), may hold values from -6 to 6
- adapter_down: bfloat16 [16, 8192, 512], P('pipe'), may hold values from -0.0625 to 0.0625
- adapter_expand: bfloat16 [16, 512, 8192], P('pipe'), may hold values from -0.25 to 0.25
- value_rows: bfloat16 [16, 32, 8192], P('pipe', 'dp'), may hold values from -0.0625 to 0.0625
- input_rows: bfloat16 [16, 32, 8192], P('pipe', 'dp'), may hold values from -0.0625 to 0.0625
- hidden_cols: bfloat16 [16, 32, 512], P('pipe'), may hold values from -0.25 to 0.25
- inner_cols: bfloat16 [16, 32, 512], P('pipe'), may hold values from -0.25 to 0.25
- lengths: int32 [32], P('dp'), may hold values from 1 to 128, as said below
- query_example: int32 [32], replicated, may hold values from 0 to 31
Outputs:
- scores: float32 [32, 32], P('dp')
Inputs may be any that keep to these rules, and one draw needn't show every extreme that they name: `lengths`: live tokens of each example; the rest of its 128 positions is padding.
All inputs are finite; a program needn't handle non-finite values.
Results may differ from a plain program's by a relative error of at most 0.022.
Values may be sent and summed in bfloat16 or wider, within the bound.
A program may use at most 128 MiB of HBM per device.

v0:
```python
import jax
import jax.numpy as jnp
from jax import lax
from jax.sharding import PartitionSpec as P

SLOT = 128
adapter_scale = 0.25


def from_behind(value, axis, steps):
    count = lax.axis_size(axis)
    first, last = (max(0, -steps), min(count, count - steps))
    return lax.ppermute(value, axis, [(source, source + steps) for source in range(first, last)])


def local(
    activations,
    cotangent,
    adapter_down,
    adapter_expand,
    value_rows,
    input_rows,
    hidden_cols,
    inner_cols,
    lengths,
    query_example,
):
    section_total = lax.axis_size("pipe")
    section_index = lax.axis_index("pipe")
    tok_dev = activations.shape[1]
    ex_dev = tok_dev // SLOT
    query_total = hidden_cols.shape[1]
    value_all, input_all = (
        lax.all_gather(value_rows[0], "dp", axis=0, tiled=True),
        lax.all_gather(input_rows[0], "dp", axis=0, tiled=True),
    )
    down_map = adapter_down[0]
    up_map = adapter_expand[0]
    hid_factor = hidden_cols[0]
    inn_factor = inner_cols[0]
    act_local = activations[0]
    block_rows = SLOT
    block_count = tok_dev // block_rows
    step_count = block_count + section_total - 1
    is_last = section_index == section_total - 1

    def advance(step_index, carry):
        incoming, per_token = carry
        block_index = step_index - (section_total - 1 - section_index)
        is_valid = (block_index >= 0) & (block_index < block_count)
        row_start = jnp.clip(block_index, 0, block_count - 1) * block_rows
        seed_rows = lax.dynamic_slice_in_dim(cotangent, row_start, block_rows, 0)
        gradient_leaving = jnp.where(is_last, seed_rows, incoming)

        def compute(unused):
            act_rows = lax.dynamic_slice_in_dim(act_local, row_start, block_rows, 0)
            hidden = jnp.dot(act_rows, down_map, preferred_element_type=jnp.float32).astype(
                jnp.bfloat16
            )
            inner_gradient = (
                adapter_scale
                * jnp.einsum(
                    "td,rd->tr", gradient_leaving, up_map, preferred_element_type=jnp.float32
                )
            ).astype(jnp.bfloat16)
            gradient_entering = (
                gradient_leaving.astype(jnp.float32)
                + jnp.einsum(
                    "tr,dr->td", inner_gradient, down_map, preferred_element_type=jnp.float32
                )
            ).astype(jnp.bfloat16)
            hidden_projection = jnp.einsum(
                "tr,qr->tq", hidden, hid_factor, preferred_element_type=jnp.float32
            )
            value_projection = jnp.einsum(
                "td,qd->tq", gradient_leaving, value_all, preferred_element_type=jnp.float32
            )
            input_projection = jnp.einsum(
                "td,qd->tq", act_rows, input_all, preferred_element_type=jnp.float32
            )
            inner_projection = jnp.einsum(
                "tr,qr->tq", inner_gradient, inn_factor, preferred_element_type=jnp.float32
            )
            return (
                gradient_entering,
                adapter_scale * hidden_projection * value_projection
                + input_projection * inner_projection,
            )

        def skipped(unused):
            return (
                jnp.zeros_like(gradient_leaving),
                jnp.zeros((block_rows, query_total), jnp.float32),
            )

        gradient_entering, summand_rows = lax.cond(is_valid, compute, skipped, 0)
        previous = lax.dynamic_slice_in_dim(per_token, row_start, block_rows, 0)
        per_token = lax.dynamic_update_slice_in_dim(
            per_token, previous + summand_rows, row_start, 0
        )
        incoming = from_behind(gradient_entering, "pipe", -1)
        return (incoming, per_token)

    start_grad = jnp.zeros((block_rows, act_local.shape[1]), jnp.bfloat16)
    start_terms = jnp.zeros((tok_dev, query_total), jnp.float32)
    final_grad, per_token = lax.fori_loop(0, step_count, advance, (start_grad, start_terms))
    offsets = lax.broadcasted_iota(jnp.int32, (tok_dev,), 0) % SLOT
    live_mask = (offsets < jnp.repeat(lengths, SLOT, total_repeat_length=tok_dev)).astype(
        jnp.float32
    )
    masked = per_token * live_mask[:, None]
    local_sums = jnp.sum(masked.reshape(ex_dev, SLOT, query_total), axis=1)
    totals = lax.psum(local_sums, "pipe") * SLOT ** (-0.5)
    example_ids = lax.axis_index("dp") * ex_dev + lax.broadcasted_iota(jnp.int32, (ex_dev,), 0)
    keep_mask = (example_ids[:, None] != query_example[None, :]).astype(jnp.float32)
    return totals * keep_mask


def solution(mesh):
    in_specs = (
        P("pipe", "dp", None),
        P("dp", None),
        P("pipe", None, None),
        P("pipe", None, None),
        P("pipe", "dp", None),
        P("pipe", "dp", None),
        P("pipe", None, None),
        P("pipe", None, None),
        P("dp"),
        P(),
    )
    out_specs = P("dp", None)
    return jax.shard_map(local, mesh=mesh, in_specs=in_specs, out_specs=out_specs, check_vma=False)
```

profile of v0, /device:TPU:8, one launch (start us, length us, event | category | flops | bytes accessed | tf_op | source)
XLA Modules:
  0.0 913.3 jit_solution(10851682348993537943)
XLA Ops:
  1.0 31.1 %all-gather = bf16[1,32,8192]{2,0,1:T(2,128)(2,1)S(1)} all-gather(bf16[1,4,8192]{2,0,1:T(2,128)(2,1)S(1)} %copy.14), channel_id=2, replica_groups=mesh['dp'=8,'pipe'=16] {'dp'}, dimensions={1}, use_global_device_ids=true | all-gather | bytes 589824 | tf_op jit(solution)/shard_map/all_gather | solution.py:34
  32.7 30.5 %all-gather.1 = bf16[1,32,8192]{2,0,1:T(2,128)(2,1)S(1)} all-gather(bf16[1,4,8192]{2,0,1:T(2,128)(2,1)S(1)} %copy.15), channel_id=3, replica_groups=mesh['dp'=8,'pipe'=16] {'dp'}, dimensions={1}, use_global_device_ids=true | all-gather | bytes 589824 | tf_op jit(solution)/shard_map/all_gather | solution.py:35
  64.1 758.5 %while.18 = (s32[]{:T(128)}, bf16[128,8192]{1,0:T(8,128)(2,1)S(1)}, f32[512,32]{0,1:T(8,128)S(1)}, s32[]{:T(128)}, pred[]{:T(512)}, /*index=5*/bf16[512,8192]{1,...) while((s32[]{:T(128)}, bf16[128,8192]{1,0:T(8,128)(2,1)S(1)}, ...), condition=%wide.region_3.4_spmd, body=%wide.region_0.3_spmd.sunk | while | flops 3368243200 | bytes 79266320 | solution.py:106
  74.8 25.6 %collective-permute-done = bf16[128,8192]{1,0:T(8,128)(2,1)S(1)} collective-permute-done((bf16[128,8192]{1,0:T(8,128)(2,1)}, bf16[128,8192]{1,0:T(8,128)(2,1)S(1)}, u32[]{:S(2)}, u32[]{:S(2)}) %collective-permute-start) | collective-permute-done | bytes 2097184 | tf_op jit(solution)/shard_map/while/body/eval_jaxpr/ppermute | solution.py:13
  103.3 26.2 %collective-permute-done = bf16[128,8192]{1,0:T(8,128)(2,1)S(1)} collective-permute-done((bf16[128,8192]{1,0:T(8,128)(2,1)}, bf16[128,8192]{1,0:T(8,128)(2,1)S(1)}, u32[]{:S(2)}, u32[]{:S(2)}) %collective-permute-start) | collective-permute-done | bytes 2097184 | tf_op jit(solution)/shard_map/while/body/eval_jaxpr/ppermute | solution.py:13
  132.4 26.2 %collective-permute-done = bf16[128,8192]{1,0:T(8,128)(2,1)S(1)} collective-permute-done((bf16[128,8192]{1,0:T(8,128)(2,1)}, bf16[128,8192]{1,0:T(8,128)(2,1)S(1)}, u32[]{:S(2)}, u32[]{:S(2)}) %collective-permute-start) | collective-permute-done | bytes 2097184 | tf_op jit(solution)/shard_map/while/body/eval_jaxpr/ppermute | solution.py:13
  161.5 26.2 %collective-permute-done = bf16[128,8192]{1,0:T(8,128)(2,1)S(1)} collective-permute-done((bf16[128,8192]{1,0:T(8,128)(2,1)}, bf16[128,8192]{1,0:T(8,128)(2,1)S(1)}, u32[]{:S(2)}, u32[]{:S(2)}) %collective-permute-start) | collective-permute-done | bytes 2097184 | tf_op jit(solution)/shard_map/while/body/eval_jaxpr/ppermute | solution.py:13
  190.6 26.2 %collective-permute-done = bf16[128,8192]{1,0:T(8,128)(2,1)S(1)} collective-permute-done((bf16[128,8192]{1,0:T(8,128)(2,1)}, bf16[128,8192]{1,0:T(8,128)(2,1)S(1)}, u32[]{:S(2)}, u32[]{:S(2)}) %collective-permute-start) | collective-permute-done | bytes 2097184 | tf_op jit(solution)/shard_map/while/body/eval_jaxpr/ppermute | solution.py:13
  219.7 26.2 %collective-permute-done = bf16[128,8192]{1,0:T(8,128)(2,1)S(1)} collective-permute-done((bf16[128,8192]{1,0:T(8,128)(2,1)}, bf16[128,8192]{1,0:T(8,128)(2,1)S(1)}, u32[]{:S(2)}, u32[]{:S(2)}) %collective-permute-start) | collective-permute-done | bytes 2097184 | tf_op jit(solution)/shard_map/while/body/eval_jaxpr/ppermute | solution.py:13
  248.8 26.2 %collective-permute-done = bf16[128,8192]{1,0:T(8,128)(2,1)S(1)} collective-permute-done((bf16[128,8192]{1,0:T(8,128)(2,1)}, bf16[128,8192]{1,0:T(8,128)(2,1)S(1)}, u32[]{:S(2)}, u32[]{:S(2)}) %collective-permute-start) | collective-permute-done | bytes 2097184 | tf_op jit(solution)/shard_map/while/body/eval_jaxpr/ppermute | solution.py:13
  277.9 26.2 %collective-permute-done = bf16[128,8192]{1,0:T(8,128)(2,1)S(1)} collective-permute-done((bf16[128,8192]{1,0:T(8,128)(2,1)}, bf16[128,8192]{1,0:T(8,128)(2,1)S(1)}, u32[]{:S(2)}, u32[]{:S(2)}) %collective-permute-start) | collective-permute-done | bytes 2097184 | tf_op jit(solution)/shard_map/while/body/eval_jaxpr/ppermute | solution.py:13
  307.0 26.2 %collective-permute-done = bf16[128,8192]{1,0:T(8,128)(2,1)S(1)} collective-permute-done((bf16[128,8192]{1,0:T(8,128)(2,1)}, bf16[128,8192]{1,0:T(8,128)(2,1)S(1)}, u32[]{:S(2)}, u32[]{:S(2)}) %collective-permute-start) | collective-permute-done | bytes 2097184 | tf_op jit(solution)/shard_map/while/body/eval_jaxpr/ppermute | solution.py:13
  336.1 26.2 %collective-permute-done = bf16[128,8192]{1,0:T(8,128)(2,1)S(1)} collective-permute-done((bf16[128,8192]{1,0:T(8,128)(2,1)}, bf16[128,8192]{1,0:T(8,128)(2,1)S(1)}, u32[]{:S(2)}, u32[]{:S(2)}) %collective-permute-start) | collective-permute-done | bytes 2097184 | tf_op jit(solution)/shard_map/while/body/eval_jaxpr/ppermute | solution.py:13
  365.2 26.2 %collective-permute-done = bf16[128,8192]{1,0:T(8,128)(2,1)S(1)} collective-permute-done((bf16[128,8192]{1,0:T(8,128)(2,1)}, bf16[128,8192]{1,0:T(8,128)(2,1)S(1)}, u32[]{:S(2)}, u32[]{:S(2)}) %collective-permute-start) | collective-permute-done | bytes 2097184 | tf_op jit(solution)/shard_map/while/body/eval_jaxpr/ppermute | solution.py:13
  394.3 26.2 %collective-permute-done = bf16[128,8192]{1,0:T(8,128)(2,1)S(1)} collective-permute-done((bf16[128,8192]{1,0:T(8,128)(2,1)}, bf16[128,8192]{1,0:T(8,128)(2,1)S(1)}, u32[]{:S(2)}, u32[]{:S(2)}) %collective-permute-start) | collective-permute-done | bytes 2097184 | tf_op jit(solution)/shard_map/while/body/eval_jaxpr/ppermute | solution.py:13
  423.4 26.2 %collective-permute-done = bf16[128,8192]{1,0:T(8,128)(2,1)S(1)} collective-permute-done((bf16[128,8192]{1,0:T(8,128)(2,1)}, bf16[128,8192]{1,0:T(8,128)(2,1)S(1)}, u32[]{:S(2)}, u32[]{:S(2)}) %collective-permute-start) | collective-permute-done | bytes 2097184 | tf_op jit(solution)/shard_map/while/body/eval_jaxpr/ppermute | solution.py:13
  452.5 182.0 %collective-permute-done = bf16[128,8192]{1,0:T(8,128)(2,1)S(1)} collective-permute-done((bf16[128,8192]{1,0:T(8,128)(2,1)}, bf16[128,8192]{1,0:T(8,128)(2,1)S(1)}, u32[]{:S(2)}, u32[]{:S(2)}) %collective-permute-start) | collective-permute-done | bytes 2097184 | tf_op jit(solution)/shard_map/while/body/eval_jaxpr/ppermute | solution.py:13
  634.5 22.1 %conditional.2 = (bf16[128,8192]{1,0:T(8,128)(2,1)}, f32[128,32]{0,1:T(8,128)S(1)}) conditional(s32[]{:T(128)} %convert_element_type.46, () %tuple.54, (pred[]{:T(512)}, bf16[512,8192]{1,0:T(8,128)(2,1)}, s32[]{:T(128)}, bf16[128,8192]{1,0:T(8,128)(2,1)S(1)}, bf16[512,8192]{1,0:T(8,128)(2,1)}, /*index=5*/bf16[8192,512]{1,0:T(8,128)(2,1)}, s32[]{:T(128)}, ...), branch_computations={%region_1.1_spmd, %region_2.2_spmd} | conditional | flops 3368239104 | bytes 70828144 | solution.py:96
  637.1 6.5 fusion.5
  648.6 5.5 fusion.15
  657.9 29.9 %collective-permute-done = bf16[128,8192]{1,0:T(8,128)(2,1)S(1)} collective-permute-done((bf16[128,8192]{1,0:T(8,128)(2,1)}, bf16[128,8192]{1,0:T(8,128)(2,1)S(1)}, u32[]{:S(2)}, u32[]{:S(2)}) %collective-permute-start) | collective-permute-done | bytes 2097184 | tf_op jit(solution)/shard_map/while/body/eval_jaxpr/ppermute | solution.py:13
  687.8 22.1 %conditional.2 = (bf16[128,8192]{1,0:T(8,128)(2,1)}, f32[128,32]{0,1:T(8,128)S(1)}) conditional(s32[]{:T(128)} %convert_element_type.46, () %tuple.54, (pred[]{:T(512)}, bf16[512,8192]{1,0:T(8,128)(2,1)}, s32[]{:T(128)}, bf16[128,8192]{1,0:T(8,128)(2,1)S(1)}, bf16[512,8192]{1,0:T(8,128)(2,1)}, /*index=5*/bf16[8192,512]{1,0:T(8,128)(2,1)}, s32[]{:T(128)}, ...), branch_computations={%region_1.1_spmd, %region_2.2_spmd} | conditional | flops 3368239104 | bytes 70828144 | solution.py:96
  690.3 6.5 fusion.5
  701.8 5.5 fusion.15
  711.2 29.9 %collective-permute-done = bf16[128,8192]{1,0:T(8,128)(2,1)S(1)} collective-permute-done((bf16[128,8192]{1,0:T(8,128)(2,1)}, bf16[128,8192]{1,0:T(8,128)(2,1)S(1)}, u32[]{:S(2)}, u32[]{:S(2)}) %collective-permute-start) | collective-permute-done | bytes 2097184 | tf_op jit(solution)/shard_map/while/body/eval_jaxpr/ppermute | solution.py:13
  741.0 22.1 %conditional.2 = (bf16[128,8192]{1,0:T(8,128)(2,1)}, f32[128,32]{0,1:T(8,128)S(1)}) conditional(s32[]{:T(128)} %convert_element_type.46, () %tuple.54, (pred[]{:T(512)}, bf16[512,8192]{1,0:T(8,128)(2,1)}, s32[]{:T(128)}, bf16[128,8192]{1,0:T(8,128)(2,1)S(1)}, bf16[512,8192]{1,0:T(8,128)(2,1)}, /*index=5*/bf16[8192,512]{1,0:T(8,128)(2,1)}, s32[]{:T(128)}, ...), branch_computations={%region_1.1_spmd, %region_2.2_spmd} | conditional | flops 3368239104 | bytes 70828144 | solution.py:96
  743.6 6.5 fusion.5
  764.4 29.0 %collective-permute-done = bf16[128,8192]{1,0:T(8,128)(2,1)S(1)} collective-permute-done((bf16[128,8192]{1,0:T(8,128)(2,1)}, bf16[128,8192]{1,0:T(8,128)(2,1)S(1)}, u32[]{:S(2)}, u32[]{:S(2)}) %collective-permute-start) | collective-permute-done | bytes 2097184 | tf_op jit(solution)/shard_map/while/body/eval_jaxpr/ppermute | solution.py:13
  793.5 22.0 %conditional.2 = (bf16[128,8192]{1,0:T(8,128)(2,1)}, f32[128,32]{0,1:T(8,128)S(1)}) conditional(s32[]{:T(128)} %convert_element_type.46, () %tuple.54, (pred[]{:T(512)}, bf16[512,8192]{1,0:T(8,128)(2,1)}, s32[]{:T(128)}, bf16[128,8192]{1,0:T(8,128)(2,1)S(1)}, bf16[512,8192]{1,0:T(8,128)(2,1)}, /*index=5*/bf16[8192,512]{1,0:T(8,128)(2,1)}, s32[]{:T(128)}, ...), branch_computations={%region_1.1_spmd, %region_2.2_spmd} | conditional | flops 3368239104 | bytes 70828144 | solution.py:96
  796.0 6.5 fusion.5
  816.8 5.8 collective-permute-done
  826.0 86.6 %psum.7 = f32[4,32]{0,1:T(8,128)S(1)} all-reduce(f32[4,32]{0,1:T(8,128)S(1)} %reduce_sum.9), channel_id=1, replica_groups=mesh['dp'=8,'pipe'=16] {'pipe'}, use_global_device_ids=true, to_apply=%region_5.6 | all-reduce | flops 128 | bytes 1024 | tf_op jit(solution)/shard_map/psum | solution.py:113
  (153 shorter events, 133.9 us)
Async XLA Ops:
  0.0 32.6 %copy-start.2 = (bf16[1,4,8192]{2,1,0:T(4,128)(2,1)S(1)}, bf16[1,4,8192]{2,1,0:T(4,128)(2,1)}, u32[]{:S(2)}) copy-start(bf16[1,4,8192]{2,1,0:T(4,128)(2,1)} %param.21) | copy-start | bytes 196612
  63.3 0.8 copy-start
  63.3 0.8 copy-start.1
  64.1 758.5 %copy-start.3 = (s32[4]{0:T(128)S(1)}, s32[4]{0:T(128)}, u32[]{:S(2)}) copy-start(s32[4]{0:T(128)} %param.24) | copy-start | bytes 52
  64.1 848.5 %copy-start.4 = (s32[32]{0:T(128)S(1)}, s32[32]{0:T(128)}, u32[]{:S(2)}) copy-start(s32[32]{0:T(128)} %param.25) | copy-start | bytes 388
  65.7 6.3 collective-permute-start
  73.5 26.9 %collective-permute-start = (bf16[128,8192]{1,0:T(8,128)(2,1)}, bf16[128,8192]{1,0:T(8,128)(2,1)S(1)}, u32[]{:S(2)}, u32[]{:S(2)}) collective-permute-start(bf16[128,8192]{1,0:T(8,128)(2,1)} %get-tuple-element.491), channel_id=1, source_target_pairs={{1,0},{2,1},{3,2},{4,3},{5,4},{6,5},{7,6},{8,7},{9,8},{10,9},{11,1... | collective-permute-start | bytes 6291464 | tf_op jit(solution)/shard_map/while/body/eval_jaxpr/ppermute | solution.py:13
  102.0 27.6 %collective-permute-start = (bf16[128,8192]{1,0:T(8,128)(2,1)}, bf16[128,8192]{1,0:T(8,128)(2,1)S(1)}, u32[]{:S(2)}, u32[]{:S(2)}) collective-permute-start(bf16[128,8192]{1,0:T(8,128)(2,1)} %get-tuple-element.491), channel_id=1, source_target_pairs={{1,0},{2,1},{3,2},{4,3},{5,4},{6,5},{7,6},{8,7},{9,8},{10,9},{11,1... | collective-permute-start | bytes 6291464 | tf_op jit(solution)/shard_map/while/body/eval_jaxpr/ppermute | solution.py:13
  131.1 27.6 %collective-permute-start = (bf16[128,8192]{1,0:T(8,128)(2,1)}, bf16[128,8192]{1,0:T(8,128)(2,1)S(1)}, u32[]{:S(2)}, u32[]{:S(2)}) collective-permute-start(bf16[128,8192]{1,0:T(8,128)(2,1)} %get-tuple-element.491), channel_id=1, source_target_pairs={{1,0},{2,1},{3,2},{4,3},{5,4},{6,5},{7,6},{8,7},{9,8},{10,9},{11,1... | collective-permute-start | bytes 6291464 | tf_op jit(solution)/shard_map/while/body/eval_jaxpr/ppermute | solution.py:13
  160.2 27.6 %collective-permute-start = (bf16[128,8192]{1,0:T(8,128)(2,1)}, bf16[128,8192]{1,0:T(8,128)(2,1)S(1)}, u32[]{:S(2)}, u32[]{:S(2)}) collective-permute-start(bf16[128,8192]{1,0:T(8,128)(2,1)} %get-tuple-element.491), channel_id=1, source_target_pairs={{1,0},{2,1},{3,2},{4,3},{5,4},{6,5},{7,6},{8,7},{9,8},{10,9},{11,1... | collective-permute-start | bytes 6291464 | tf_op jit(solution)/shard_map/while/body/eval_jaxpr/ppermute | solution.py:13
  189.3 27.6 %collective-permute-start = (bf16[128,8192]{1,0:T(8,128)(2,1)}, bf16[128,8192]{1,0:T(8,128)(2,1)S(1)}, u32[]{:S(2)}, u32[]{:S(2)}) collective-permute-start(bf16[128,8192]{1,0:T(8,128)(2,1)} %get-tuple-element.491), channel_id=1, source_target_pairs={{1,0},{2,1},{3,2},{4,3},{5,4},{6,5},{7,6},{8,7},{9,8},{10,9},{11,1... | collective-permute-start | bytes 6291464 | tf_op jit(solution)/shard_map/while/body/eval_jaxpr/ppermute | solution.py:13
  218.4 27.6 %collective-permute-start = (bf16[128,8192]{1,0:T(8,128)(2,1)}, bf16[128,8192]{1,0:T(8,128)(2,1)S(1)}, u32[]{:S(2)}, u32[]{:S(2)}) collective-permute-start(bf16[128,8192]{1,0:T(8,128)(2,1)} %get-tuple-element.491), channel_id=1, source_target_pairs={{1,0},{2,1},{3,2},{4,3},{5,4},{6,5},{7,6},{8,7},{9,8},{10,9},{11,1... | collective-permute-start | bytes 6291464 | tf_op jit(solution)/shard_map/while/body/eval_jaxpr/ppermute | solution.py:13
  247.5 27.6 %collective-permute-start = (bf16[128,8192]{1,0:T(8,128)(2,1)}, bf16[128,8192]{1,0:T(8,128)(2,1)S(1)}, u32[]{:S(2)}, u32[]{:S(2)}) collective-permute-start(bf16[128,8192]{1,0:T(8,128)(2,1)} %get-tuple-element.491), channel_id=1, source_target_pairs={{1,0},{2,1},{3,2},{4,3},{5,4},{6,5},{7,6},{8,7},{9,8},{10,9},{11,1... | collective-permute-start | bytes 6291464 | tf_op jit(solution)/shard_map/while/body/eval_jaxpr/ppermute | solution.py:13
  276.6 27.6 %collective-permute-start = (bf16[128,8192]{1,0:T(8,128)(2,1)}, bf16[128,8192]{1,0:T(8,128)(2,1)S(1)}, u32[]{:S(2)}, u32[]{:S(2)}) collective-permute-start(bf16[128,8192]{1,0:T(8,128)(2,1)} %get-tuple-element.491), channel_id=1, source_target_pairs={{1,0},{2,1},{3,2},{4,3},{5,4},{6,5},{7,6},{8,7},{9,8},{10,9},{11,1... | collective-permute-start | bytes 6291464 | tf_op jit(solution)/shard_map/while/body/eval_jaxpr/ppermute | solution.py:13
  305.7 27.6 %collective-permute-start = (bf16[128,8192]{1,0:T(8,128)(2,1)}, bf16[128,8192]{1,0:T(8,128)(2,1)S(1)}, u32[]{:S(2)}, u32[]{:S(2)}) collective-permute-start(bf16[128,8192]{1,0:T(8,128)(2,1)} %get-tuple-element.491), channel_id=1, source_target_pairs={{1,0},{2,1},{3,2},{4,3},{5,4},{6,5},{7,6},{8,7},{9,8},{10,9},{11,1... | collective-permute-start | bytes 6291464 | tf_op jit(solution)/shard_map/while/body/eval_jaxpr/ppermute | solution.py:13
  334.8 27.6 %collective-permute-start = (bf16[128,8192]{1,0:T(8,128)(2,1)}, bf16[128,8192]{1,0:T(8,128)(2,1)S(1)}, u32[]{:S(2)}, u32[]{:S(2)}) collective-permute-start(bf16[128,8192]{1,0:T(8,128)(2,1)} %get-tuple-element.491), channel_id=1, source_target_pairs={{1,0},{2,1},{3,2},{4,3},{5,4},{6,5},{7,6},{8,7},{9,8},{10,9},{11,1... | collective-permute-start | bytes 6291464 | tf_op jit(solution)/shard_map/while/body/eval_jaxpr/ppermute | solution.py:13
  363.9 27.6 %collective-permute-start = (bf16[128,8192]{1,0:T(8,128)(2,1)}, bf16[128,8192]{1,0:T(8,128)(2,1)S(1)}, u32[]{:S(2)}, u32[]{:S(2)}) collective-permute-start(bf16[128,8192]{1,0:T(8,128)(2,1)} %get-tuple-element.491), channel_id=1, source_target_pairs={{1,0},{2,1},{3,2},{4,3},{5,4},{6,5},{7,6},{8,7},{9,8},{10,9},{11,1... | collective-permute-start | bytes 6291464 | tf_op jit(solution)/shard_map/while/body/eval_jaxpr/ppermute | solution.py:13
  393.0 27.6 %collective-permute-start = (bf16[128,8192]{1,0:T(8,128)(2,1)}, bf16[128,8192]{1,0:T(8,128)(2,1)S(1)}, u32[]{:S(2)}, u32[]{:S(2)}) collective-permute-start(bf16[128,8192]{1,0:T(8,128)(2,1)} %get-tuple-element.491), channel_id=1, source_target_pairs={{1,0},{2,1},{3,2},{4,3},{5,4},{6,5},{7,6},{8,7},{9,8},{10,9},{11,1... | collective-permute-start | bytes 6291464 | tf_op jit(solution)/shard_map/while/body/eval_jaxpr/ppermute | solution.py:13
  422.1 27.6 %collective-permute-start = (bf16[128,8192]{1,0:T(8,128)(2,1)}, bf16[128,8192]{1,0:T(8,128)(2,1)S(1)}, u32[]{:S(2)}, u32[]{:S(2)}) collective-permute-start(bf16[128,8192]{1,0:T(8,128)(2,1)} %get-tuple-element.491), channel_id=1, source_target_pairs={{1,0},{2,1},{3,2},{4,3},{5,4},{6,5},{7,6},{8,7},{9,8},{10,9},{11,1... | collective-permute-start | bytes 6291464 | tf_op jit(solution)/shard_map/while/body/eval_jaxpr/ppermute | solution.py:13
  451.2 183.3 %collective-permute-start = (bf16[128,8192]{1,0:T(8,128)(2,1)}, bf16[128,8192]{1,0:T(8,128)(2,1)S(1)}, u32[]{:S(2)}, u32[]{:S(2)}) collective-permute-start(bf16[128,8192]{1,0:T(8,128)(2,1)} %get-tuple-element.491), channel_id=1, source_target_pairs={{1,0},{2,1},{3,2},{4,3},{5,4},{6,5},{7,6},{8,7},{9,8},{10,9},{11,1... | collective-permute-start | bytes 6291464 | tf_op jit(solution)/shard_map/while/body/eval_jaxpr/ppermute | solution.py:13
  634.5 9.0 slice-start
  637.0 6.5 slice-start.1
  656.6 31.2 %collective-permute-start = (bf16[128,8192]{1,0:T(8,128)(2,1)}, bf16[128,8192]{1,0:T(8,128)(2,1)S(1)}, u32[]{:S(2)}, u32[]{:S(2)}) collective-permute-start(bf16[128,8192]{1,0:T(8,128)(2,1)} %get-tuple-element.491), channel_id=1, source_target_pairs={{1,0},{2,1},{3,2},{4,3},{5,4},{6,5},{7,6},{8,7},{9,8},{10,9},{11,1... | collective-permute-start | bytes 6291464 | tf_op jit(solution)/shard_map/while/body/eval_jaxpr/ppermute | solution.py:13
  687.8 9.0 slice-start
  690.3 6.5 slice-start.1
  709.8 31.2 %collective-permute-start = (bf16[128,8192]{1,0:T(8,128)(2,1)}, bf16[128,8192]{1,0:T(8,128)(2,1)S(1)}, u32[]{:S(2)}, u32[]{:S(2)}) collective-permute-start(bf16[128,8192]{1,0:T(8,128)(2,1)} %get-tuple-element.491), channel_id=1, source_target_pairs={{1,0},{2,1},{3,2},{4,3},{5,4},{6,5},{7,6},{8,7},{9,8},{10,9},{11,1... | collective-permute-start | bytes 6291464 | tf_op jit(solution)/shard_map/while/body/eval_jaxpr/ppermute | solution.py:13
  741.0 9.0 slice-start
  743.6 6.5 slice-start.1
  763.1 30.4 %collective-permute-start = (bf16[128,8192]{1,0:T(8,128)(2,1)}, bf16[128,8192]{1,0:T(8,128)(2,1)S(1)}, u32[]{:S(2)}, u32[]{:S(2)}) collective-permute-start(bf16[128,8192]{1,0:T(8,128)(2,1)} %get-tuple-element.491), channel_id=1, source_target_pairs={{1,0},{2,1},{3,2},{4,3},{5,4},{6,5},{7,6},{8,7},{9,8},{10,9},{11,1... | collective-permute-start | bytes 6291464 | tf_op jit(solution)/shard_map/while/body/eval_jaxpr/ppermute | solution.py:13
  793.5 9.0 slice-start
  796.0 6.5 slice-start.1
  815.4 7.2 collective-permute-start
where the time goes:
time: 914 us; the launch traced here: 913 us
  waiting for transfers between devices  622 us (68%)
  blocking collectives  148 us (16%)
  matrix products  77.8 us (9%)
  local copies, waits for them, and re-layouts  27.1 us (3%)
  starting transfers between devices  24.4 us (3%)
  other arithmetic  13.2 us (1%)
    ppermute x19, waiting for transfers between devices, from_behind(): lax.ppermute(value, axis, [(source, source + steps) for source in range(f...  622 us
    psum x1, blocking collectives, local(): totals = lax.psum(local_sums, 'pipe') * SLOT ** (-0.5)  86.6 us
    all_gather x1, blocking collectives, local(): lax.all_gather(value_rows[0], 'dp', axis=0, tiled=True)  31.1 us
    all_gather x1, blocking collectives, local(): lax.all_gather(input_rows[0], 'dp', axis=0, tiled=True)  30.5 us
    dot_general x4, matrix products, compute(): jnp.einsum('td,rd->tr', gradient_leaving, up_map, preferred_element_type=...  25.8 us
    ppermute x19, starting transfers between devices, from_behind(): lax.ppermute(value, axis, [(source, source + steps) for source in range(f...  24.4 us
    another operation x31, local copies, waits for them, and re-layouts  23.5 us
    dot_general x4, matrix products, compute(): jnp.einsum('tr,qr->tq', hidden, hid_factor, preferred_element_type=jnp.fl...  21.8 us
  transfers between devices with their start and end apart: 19, of which 19 were waited for; matrix products, arithmetic and copies ran while one was open for 0% of the time, Pallas kernels for 0%

commit v1 on v0

--- a/solution.py
+++ b/solution.py
@@ -110,7 +110,7 @@
     )
     masked = per_token * live_mask[:, None]
     local_sums = jnp.sum(masked.reshape(ex_dev, SLOT, query_total), axis=1)
-    totals = lax.psum(local_sums, "pipe") * SLOT ** (-0.5)
+    totals = jnp.sum(lax.all_gather(local_sums, "pipe"), axis=0) * SLOT ** (-0.5)
     example_ids = lax.axis_index("dp") * ex_dev + lax.broadcasted_iota(jnp.int32, (ex_dev,), 0)
     keep_mask = (example_ids[:, None] != query_example[None, :]).astype(jnp.float32)
     return totals * keep_mask

time: 914 us -> 869 us (0.951)
  blocking collectives: 148 us -> 102 us
    psum x1 -> x0, blocking collectives: 86.6 us -> none  [local(): totals = lax.psum(local_sums, 'pipe') * SLOT ** (-0.5)]
    all_gather x0 -> x1, blocking collectives: none -> 40.8 us  [local(): lax.all_gather(local_sums, 'pipe')]
where the time goes in v1:
time: 869 us; the launch traced here: 868 us
  waiting for transfers between devices  622 us (72%)
  blocking collectives  102 us (12%)
  matrix products  77.8 us (9%)
  local copies, waits for them, and re-layouts  26.5 us (3%)
  starting transfers between devices  24.4 us (3%)
  other arithmetic  13.8 us (2%)
    ppermute x19, waiting for transfers between devices, from_behind(): lax.ppermute(value, axis, [(source, source + steps) for source in range(f...  622 us
    all_gather x1, blocking collectives, local(): lax.all_gather(local_sums, 'pipe')  40.8 us
    all_gather x1, blocking collectives, local(): lax.all_gather(value_rows[0], 'dp', axis=0, tiled=True)  31.1 us
    all_gather x1, blocking collectives, local(): lax.all_gather(input_rows[0], 'dp', axis=0, tiled=True)  30.5 us
    dot_general x4, matrix products, compute(): jnp.einsum('td,rd->tr', gradient_leaving, up_map, preferred_element_type=...  25.8 us
    ppermute x19, starting transfers between devices, from_behind(): lax.ppermute(value, axis, [(source, source + steps) for source in range(f...  24.4 us
    another operation x31, local copies, waits for them, and re-layouts  23.5 us
    dot_general x4, matrix products, compute(): jnp.einsum('tr,qr->tq', hidden, hid_factor, preferred_element_type=jnp.fl...  21.8 us
  transfers between devices with their start and end apart: 19, of which 19 were waited for; matrix products, arithmetic and copies ran while one was open for 0% of the time, Pallas kernels for 0%

profile of v1, /device:TPU:8, one launch (start us, length us, event | category | flops | bytes accessed | tf_op | source)
XLA Modules:
  0.0 867.6 jit_solution(6736437613618303772)
XLA Ops:
  1.0 31.1 %all-gather = bf16[1,32,8192]{2,0,1:T(2,128)(2,1)S(1)} all-gather(bf16[1,4,8192]{2,0,1:T(2,128)(2,1)S(1)} %copy.14), channel_id=2, replica_groups=mesh['dp'=8,'pipe'=16] {'dp'}, dimensions={1}, use_global_device_ids=true | all-gather | bytes 589824 | tf_op jit(solution)/shard_map/all_gather | solution.py:34
  32.7 30.5 %all-gather.1 = bf16[1,32,8192]{2,0,1:T(2,128)(2,1)S(1)} all-gather(bf16[1,4,8192]{2,0,1:T(2,128)(2,1)S(1)} %copy.15), channel_id=3, replica_groups=mesh['dp'=8,'pipe'=16] {'dp'}, dimensions={1}, use_global_device_ids=true | all-gather | bytes 589824 | tf_op jit(solution)/shard_map/all_gather | solution.py:35
  64.1 758.5 %while.18 = (s32[]{:T(128)}, bf16[128,8192]{1,0:T(8,128)(2,1)S(1)}, f32[512,32]{0,1:T(8,128)S(1)}, s32[]{:T(128)}, pred[]{:T(512)}, /*index=5*/bf16[512,8192]{1,...) while((s32[]{:T(128)}, bf16[128,8192]{1,0:T(8,128)(2,1)S(1)}, ...), condition=%wide.region_3.4_spmd, body=%wide.region_0.3_spmd.sunk | while | flops 3368243200 | bytes 79266320 | solution.py:106
  74.8 25.6 %collective-permute-done = bf16[128,8192]{1,0:T(8,128)(2,1)S(1)} collective-permute-done((bf16[128,8192]{1,0:T(8,128)(2,1)}, bf16[128,8192]{1,0:T(8,128)(2,1)S(1)}, u32[]{:S(2)}, u32[]{:S(2)}) %collective-permute-start) | collective-permute-done | bytes 2097184 | tf_op jit(solution)/shard_map/while/body/eval_jaxpr/ppermute | solution.py:13
  103.3 26.2 %collective-permute-done = bf16[128,8192]{1,0:T(8,128)(2,1)S(1)} collective-permute-done((bf16[128,8192]{1,0:T(8,128)(2,1)}, bf16[128,8192]{1,0:T(8,128)(2,1)S(1)}, u32[]{:S(2)}, u32[]{:S(2)}) %collective-permute-start) | collective-permute-done | bytes 2097184 | tf_op jit(solution)/shard_map/while/body/eval_jaxpr/ppermute | solution.py:13
  132.4 26.2 %collective-permute-done = bf16[128,8192]{1,0:T(8,128)(2,1)S(1)} collective-permute-done((bf16[128,8192]{1,0:T(8,128)(2,1)}, bf16[128,8192]{1,0:T(8,128)(2,1)S(1)}, u32[]{:S(2)}, u32[]{:S(2)}) %collective-permute-start) | collective-permute-done | bytes 2097184 | tf_op jit(solution)/shard_map/while/body/eval_jaxpr/ppermute | solution.py:13
  161.5 26.2 %collective-permute-done = bf16[128,8192]{1,0:T(8,128)(2,1)S(1)} collective-permute-done((bf16[128,8192]{1,0:T(8,128)(2,1)}, bf16[128,8192]{1,0:T(8,128)(2,1)S(1)}, u32[]{:S(2)}, u32[]{:S(2)}) %collective-permute-start) | collective-permute-done | bytes 2097184 | tf_op jit(solution)/shard_map/while/body/eval_jaxpr/ppermute | solution.py:13
  190.6 26.2 %collective-permute-done = bf16[128,8192]{1,0:T(8,128)(2,1)S(1)} collective-permute-done((bf16[128,8192]{1,0:T(8,128)(2,1)}, bf16[128,8192]{1,0:T(8,128)(2,1)S(1)}, u32[]{:S(2)}, u32[]{:S(2)}) %collective-permute-start) | collective-permute-done | bytes 2097184 | tf_op jit(solution)/shard_map/while/body/eval_jaxpr/ppermute | solution.py:13
  219.7 26.2 %collective-permute-done = bf16[128,8192]{1,0:T(8,128)(2,1)S(1)} collective-permute-done((bf16[128,8192]{1,0:T(8,128)(2,1)}, bf16[128,8192]{1,0:T(8,128)(2,1)S(1)}, u32[]{:S(2)}, u32[]{:S(2)}) %collective-permute-start) | collective-permute-done | bytes 2097184 | tf_op jit(solution)/shard_map/while/body/eval_jaxpr/ppermute | solution.py:13
  248.8 26.2 %collective-permute-done = bf16[128,8192]{1,0:T(8,128)(2,1)S(1)} collective-permute-done((bf16[128,8192]{1,0:T(8,128)(2,1)}, bf16[128,8192]{1,0:T(8,128)(2,1)S(1)}, u32[]{:S(2)}, u32[]{:S(2)}) %collective-permute-start) | collective-permute-done | bytes 2097184 | tf_op jit(solution)/shard_map/while/body/eval_jaxpr/ppermute | solution.py:13
  277.9 26.2 %collective-permute-done = bf16[128,8192]{1,0:T(8,128)(2,1)S(1)} collective-permute-done((bf16[128,8192]{1,0:T(8,128)(2,1)}, bf16[128,8192]{1,0:T(8,128)(2,1)S(1)}, u32[]{:S(2)}, u32[]{:S(2)}) %collective-permute-start) | collective-permute-done | bytes 2097184 | tf_op jit(solution)/shard_map/while/body/eval_jaxpr/ppermute | solution.py:13
  307.0 26.2 %collective-permute-done = bf16[128,8192]{1,0:T(8,128)(2,1)S(1)} collective-permute-done((bf16[128,8192]{1,0:T(8,128)(2,1)}, bf16[128,8192]{1,0:T(8,128)(2,1)S(1)}, u32[]{:S(2)}, u32[]{:S(2)}) %collective-permute-start) | collective-permute-done | bytes 2097184 | tf_op jit(solution)/shard_map/while/body/eval_jaxpr/ppermute | solution.py:13
  336.1 26.2 %collective-permute-done = bf16[128,8192]{1,0:T(8,128)(2,1)S(1)} collective-permute-done((bf16[128,8192]{1,0:T(8,128)(2,1)}, bf16[128,8192]{1,0:T(8,128)(2,1)S(1)}, u32[]{:S(2)}, u32[]{:S(2)}) %collective-permute-start) | collective-permute-done | bytes 2097184 | tf_op jit(solution)/shard_map/while/body/eval_jaxpr/ppermute | solution.py:13
  365.2 26.2 %collective-permute-done = bf16[128,8192]{1,0:T(8,128)(2,1)S(1)} collective-permute-done((bf16[128,8192]{1,0:T(8,128)(2,1)}, bf16[128,8192]{1,0:T(8,128)(2,1)S(1)}, u32[]{:S(2)}, u32[]{:S(2)}) %collective-permute-start) | collective-permute-done | bytes 2097184 | tf_op jit(solution)/shard_map/while/body/eval_jaxpr/ppermute | solution.py:13
  394.3 26.2 %collective-permute-done = bf16[128,8192]{1,0:T(8,128)(2,1)S(1)} collective-permute-done((bf16[128,8192]{1,0:T(8,128)(2,1)}, bf16[128,8192]{1,0:T(8,128)(2,1)S(1)}, u32[]{:S(2)}, u32[]{:S(2)}) %collective-permute-start) | collective-permute-done | bytes 2097184 | tf_op jit(solution)/shard_map/while/body/eval_jaxpr/ppermute | solution.py:13
  423.4 26.2 %collective-permute-done = bf16[128,8192]{1,0:T(8,128)(2,1)S(1)} collective-permute-done((bf16[128,8192]{1,0:T(8,128)(2,1)}, bf16[128,8192]{1,0:T(8,128)(2,1)S(1)}, u32[]{:S(2)}, u32[]{:S(2)}) %collective-permute-start) | collective-permute-done | bytes 2097184 | tf_op jit(solution)/shard_map/while/body/eval_jaxpr/ppermute | solution.py:13
  452.5 182.0 %collective-permute-done = bf16[128,8192]{1,0:T(8,128)(2,1)S(1)} collective-permute-done((bf16[128,8192]{1,0:T(8,128)(2,1)}, bf16[128,8192]{1,0:T(8,128)(2,1)S(1)}, u32[]{:S(2)}, u32[]{:S(2)}) %collective-permute-start) | collective-permute-done | bytes 2097184 | tf_op jit(solution)/shard_map/while/body/eval_jaxpr/ppermute | solution.py:13
  634.5 22.1 %conditional.2 = (bf16[128,8192]{1,0:T(8,128)(2,1)}, f32[128,32]{0,1:T(8,128)S(1)}) conditional(s32[]{:T(128)} %convert_element_type.46, () %tuple.54, (pred[]{:T(512)}, bf16[512,8192]{1,0:T(8,128)(2,1)}, s32[]{:T(128)}, bf16[128,8192]{1,0:T(8,128)(2,1)S(1)}, bf16[512,8192]{1,0:T(8,128)(2,1)}, /*index=5*/bf16[8192,512]{1,0:T(8,128)(2,1)}, s32[]{:T(128)}, ...), branch_computations={%region_1.1_spmd, %region_2.2_spmd} | conditional | flops 3368239104 | bytes 70828144 | solution.py:96
  637.1 6.5 fusion.5
  648.6 5.5 fusion.15
  657.9 29.9 %collective-permute-done = bf16[128,8192]{1,0:T(8,128)(2,1)S(1)} collective-permute-done((bf16[128,8192]{1,0:T(8,128)(2,1)}, bf16[128,8192]{1,0:T(8,128)(2,1)S(1)}, u32[]{:S(2)}, u32[]{:S(2)}) %collective-permute-start) | collective-permute-done | bytes 2097184 | tf_op jit(solution)/shard_map/while/body/eval_jaxpr/ppermute | solution.py:13
  687.8 22.1 %conditional.2 = (bf16[128,8192]{1,0:T(8,128)(2,1)}, f32[128,32]{0,1:T(8,128)S(1)}) conditional(s32[]{:T(128)} %convert_element_type.46, () %tuple.54, (pred[]{:T(512)}, bf16[512,8192]{1,0:T(8,128)(2,1)}, s32[]{:T(128)}, bf16[128,8192]{1,0:T(8,128)(2,1)S(1)}, bf16[512,8192]{1,0:T(8,128)(2,1)}, /*index=5*/bf16[8192,512]{1,0:T(8,128)(2,1)}, s32[]{:T(128)}, ...), branch_computations={%region_1.1_spmd, %region_2.2_spmd} | conditional | flops 3368239104 | bytes 70828144 | solution.py:96
  690.3 6.5 fusion.5
  701.8 5.5 fusion.15
  711.2 29.9 %collective-permute-done = bf16[128,8192]{1,0:T(8,128)(2,1)S(1)} collective-permute-done((bf16[128,8192]{1,0:T(8,128)(2,1)}, bf16[128,8192]{1,0:T(8,128)(2,1)S(1)}, u32[]{:S(2)}, u32[]{:S(2)}) %collective-permute-start) | collective-permute-done | bytes 2097184 | tf_op jit(solution)/shard_map/while/body/eval_jaxpr/ppermute | solution.py:13
  741.0 22.1 %conditional.2 = (bf16[128,8192]{1,0:T(8,128)(2,1)}, f32[128,32]{0,1:T(8,128)S(1)}) conditional(s32[]{:T(128)} %convert_element_type.46, () %tuple.54, (pred[]{:T(512)}, bf16[512,8192]{1,0:T(8,128)(2,1)}, s32[]{:T(128)}, bf16[128,8192]{1,0:T(8,128)(2,1)S(1)}, bf16[512,8192]{1,0:T(8,128)(2,1)}, /*index=5*/bf16[8192,512]{1,0:T(8,128)(2,1)}, s32[]{:T(128)}, ...), branch_computations={%region_1.1_spmd, %region_2.2_spmd} | conditional | flops 3368239104 | bytes 70828144 | solution.py:96
  743.6 6.5 fusion.5
  764.4 29.0 %collective-permute-done = bf16[128,8192]{1,0:T(8,128)(2,1)S(1)} collective-permute-done((bf16[128,8192]{1,0:T(8,128)(2,1)}, bf16[128,8192]{1,0:T(8,128)(2,1)S(1)}, u32[]{:S(2)}, u32[]{:S(2)}) %collective-permute-start) | collective-permute-done | bytes 2097184 | tf_op jit(solution)/shard_map/while/body/eval_jaxpr/ppermute | solution.py:13
  793.5 22.0 %conditional.2 = (bf16[128,8192]{1,0:T(8,128)(2,1)}, f32[128,32]{0,1:T(8,128)S(1)}) conditional(s32[]{:T(128)} %convert_element_type.46, () %tuple.54, (pred[]{:T(512)}, bf16[512,8192]{1,0:T(8,128)(2,1)}, s32[]{:T(128)}, bf16[128,8192]{1,0:T(8,128)(2,1)S(1)}, bf16[512,8192]{1,0:T(8,128)(2,1)}, /*index=5*/bf16[8192,512]{1,0:T(8,128)(2,1)}, s32[]{:T(128)}, ...), branch_computations={%region_1.1_spmd, %region_2.2_spmd} | conditional | flops 3368239104 | bytes 70828144 | solution.py:96
  796.0 6.5 fusion.5
  816.8 5.8 collective-permute-done
  826.1 40.8 %all-gather.3 = f32[16,4,32]{2,1,0:T(4,128)S(1)} all-gather(f32[1,4,32]{2,1,0:T(4,128)S(1)} %bitcast.53), channel_id=4, replica_groups=mesh['dp'=8,'pipe'=16] {'pipe'}, dimensions={0}, use_global_device_ids=true | all-gather | bytes 8704 | tf_op jit(solution)/shard_map/all_gather | solution.py:113
  (154 shorter events, 134.0 us)
Async XLA Ops:
  0.0 32.6 %copy-start.2 = (bf16[1,4,8192]{2,1,0:T(4,128)(2,1)S(1)}, bf16[1,4,8192]{2,1,0:T(4,128)(2,1)}, u32[]{:S(2)}) copy-start(bf16[1,4,8192]{2,1,0:T(4,128)(2,1)} %param.21) | copy-start | bytes 196612
  63.3 0.8 copy-start
  63.3 0.8 copy-start.1
  64.1 758.5 %copy-start.3 = (s32[4]{0:T(128)S(1)}, s32[4]{0:T(128)}, u32[]{:S(2)}) copy-start(s32[4]{0:T(128)} %param.24) | copy-start | bytes 52
  64.1 802.8 %copy-start.4 = (s32[32]{0:T(128)S(1)}, s32[32]{0:T(128)}, u32[]{:S(2)}) copy-start(s32[32]{0:T(128)} %param.25) | copy-start | bytes 388
  65.7 6.3 collective-permute-start
  73.5 26.9 %collective-permute-start = (bf16[128,8192]{1,0:T(8,128)(2,1)}, bf16[128,8192]{1,0:T(8,128)(2,1)S(1)}, u32[]{:S(2)}, u32[]{:S(2)}) collective-permute-start(bf16[128,8192]{1,0:T(8,128)(2,1)} %get-tuple-element.491), channel_id=1, source_target_pairs={{1,0},{2,1},{3,2},{4,3},{5,4},{6,5},{7,6},{8,7},{9,8},{10,9},{11,1... | collective-permute-start | bytes 6291464 | tf_op jit(solution)/shard_map/while/body/eval_jaxpr/ppermute | solution.py:13
  102.0 27.6 %collective-permute-start = (bf16[128,8192]{1,0:T(8,128)(2,1)}, bf16[128,8192]{1,0:T(8,128)(2,1)S(1)}, u32[]{:S(2)}, u32[]{:S(2)}) collective-permute-start(bf16[128,8192]{1,0:T(8,128)(2,1)} %get-tuple-element.491), channel_id=1, source_target_pairs={{1,0},{2,1},{3,2},{4,3},{5,4},{6,5},{7,6},{8,7},{9,8},{10,9},{11,1... | collective-permute-start | bytes 6291464 | tf_op jit(solution)/shard_map/while/body/eval_jaxpr/ppermute | solution.py:13
  131.1 27.6 %collective-permute-start = (bf16[128,8192]{1,0:T(8,128)(2,1)}, bf16[128,8192]{1,0:T(8,128)(2,1)S(1)}, u32[]{:S(2)}, u32[]{:S(2)}) collective-permute-start(bf16[128,8192]{1,0:T(8,128)(2,1)} %get-tuple-element.491), channel_id=1, source_target_pairs={{1,0},{2,1},{3,2},{4,3},{5,4},{6,5},{7,6},{8,7},{9,8},{10,9},{11,1... | collective-permute-start | bytes 6291464 | tf_op jit(solution)/shard_map/while/body/eval_jaxpr/ppermute | solution.py:13
  160.2 27.6 %collective-permute-start = (bf16[128,8192]{1,0:T(8,128)(2,1)}, bf16[128,8192]{1,0:T(8,128)(2,1)S(1)}, u32[]{:S(2)}, u32[]{:S(2)}) collective-permute-start(bf16[128,8192]{1,0:T(8,128)(2,1)} %get-tuple-element.491), channel_id=1, source_target_pairs={{1,0},{2,1},{3,2},{4,3},{5,4},{6,5},{7,6},{8,7},{9,8},{10,9},{11,1... | collective-permute-start | bytes 6291464 | tf_op jit(solution)/shard_map/while/body/eval_jaxpr/ppermute | solution.py:13
  189.3 27.6 %collective-permute-start = (bf16[128,8192]{1,0:T(8,128)(2,1)}, bf16[128,8192]{1,0:T(8,128)(2,1)S(1)}, u32[]{:S(2)}, u32[]{:S(2)}) collective-permute-start(bf16[128,8192]{1,0:T(8,128)(2,1)} %get-tuple-element.491), channel_id=1, source_target_pairs={{1,0},{2,1},{3,2},{4,3},{5,4},{6,5},{7,6},{8,7},{9,8},{10,9},{11,1... | collective-permute-start | bytes 6291464 | tf_op jit(solution)/shard_map/while/body/eval_jaxpr/ppermute | solution.py:13
  218.4 27.6 %collective-permute-start = (bf16[128,8192]{1,0:T(8,128)(2,1)}, bf16[128,8192]{1,0:T(8,128)(2,1)S(1)}, u32[]{:S(2)}, u32[]{:S(2)}) collective-permute-start(bf16[128,8192]{1,0:T(8,128)(2,1)} %get-tuple-element.491), channel_id=1, source_target_pairs={{1,0},{2,1},{3,2},{4,3},{5,4},{6,5},{7,6},{8,7},{9,8},{10,9},{11,1... | collective-permute-start | bytes 6291464 | tf_op jit(solution)/shard_map/while/body/eval_jaxpr/ppermute | solution.py:13
  247.5 27.6 %collective-permute-start = (bf16[128,8192]{1,0:T(8,128)(2,1)}, bf16[128,8192]{1,0:T(8,128)(2,1)S(1)}, u32[]{:S(2)}, u32[]{:S(2)}) collective-permute-start(bf16[128,8192]{1,0:T(8,128)(2,1)} %get-tuple-element.491), channel_id=1, source_target_pairs={{1,0},{2,1},{3,2},{4,3},{5,4},{6,5},{7,6},{8,7},{9,8},{10,9},{11,1... | collective-permute-start | bytes 6291464 | tf_op jit(solution)/shard_map/while/body/eval_jaxpr/ppermute | solution.py:13
  276.6 27.6 %collective-permute-start = (bf16[128,8192]{1,0:T(8,128)(2,1)}, bf16[128,8192]{1,0:T(8,128)(2,1)S(1)}, u32[]{:S(2)}, u32[]{:S(2)}) collective-permute-start(bf16[128,8192]{1,0:T(8,128)(2,1)} %get-tuple-element.491), channel_id=1, source_target_pairs={{1,0},{2,1},{3,2},{4,3},{5,4},{6,5},{7,6},{8,7},{9,8},{10,9},{11,1... | collective-permute-start | bytes 6291464 | tf_op jit(solution)/shard_map/while/body/eval_jaxpr/ppermute | solution.py:13
  305.7 27.6 %collective-permute-start = (bf16[128,8192]{1,0:T(8,128)(2,1)}, bf16[128,8192]{1,0:T(8,128)(2,1)S(1)}, u32[]{:S(2)}, u32[]{:S(2)}) collective-permute-start(bf16[128,8192]{1,0:T(8,128)(2,1)} %get-tuple-element.491), channel_id=1, source_target_pairs={{1,0},{2,1},{3,2},{4,3},{5,4},{6,5},{7,6},{8,7},{9,8},{10,9},{11,1... | collective-permute-start | bytes 6291464 | tf_op jit(solution)/shard_map/while/body/eval_jaxpr/ppermute | solution.py:13
  334.8 27.6 %collective-permute-start = (bf16[128,8192]{1,0:T(8,128)(2,1)}, bf16[128,8192]{1,0:T(8,128)(2,1)S(1)}, u32[]{:S(2)}, u32[]{:S(2)}) collective-permute-start(bf16[128,8192]{1,0:T(8,128)(2,1)} %get-tuple-element.491), channel_id=1, source_target_pairs={{1,0},{2,1},{3,2},{4,3},{5,4},{6,5},{7,6},{8,7},{9,8},{10,9},{11,1... | collective-permute-start | bytes 6291464 | tf_op jit(solution)/shard_map/while/body/eval_jaxpr/ppermute | solution.py:13
  363.9 27.6 %collective-permute-start = (bf16[128,8192]{1,0:T(8,128)(2,1)}, bf16[128,8192]{1,0:T(8,128)(2,1)S(1)}, u32[]{:S(2)}, u32[]{:S(2)}) collective-permute-start(bf16[128,8192]{1,0:T(8,128)(2,1)} %get-tuple-element.491), channel_id=1, source_target_pairs={{1,0},{2,1},{3,2},{4,3},{5,4},{6,5},{7,6},{8,7},{9,8},{10,9},{11,1... | collective-permute-start | bytes 6291464 | tf_op jit(solution)/shard_map/while/body/eval_jaxpr/ppermute | solution.py:13
  393.0 27.6 %collective-permute-start = (bf16[128,8192]{1,0:T(8,128)(2,1)}, bf16[128,8192]{1,0:T(8,128)(2,1)S(1)}, u32[]{:S(2)}, u32[]{:S(2)}) collective-permute-start(bf16[128,8192]{1,0:T(8,128)(2,1)} %get-tuple-element.491), channel_id=1, source_target_pairs={{1,0},{2,1},{3,2},{4,3},{5,4},{6,5},{7,6},{8,7},{9,8},{10,9},{11,1... | collective-permute-start | bytes 6291464 | tf_op jit(solution)/shard_map/while/body/eval_jaxpr/ppermute | solution.py:13
  422.1 27.6 %collective-permute-start = (bf16[128,8192]{1,0:T(8,128)(2,1)}, bf16[128,8192]{1,0:T(8,128)(2,1)S(1)}, u32[]{:S(2)}, u32[]{:S(2)}) collective-permute-start(bf16[128,8192]{1,0:T(8,128)(2,1)} %get-tuple-element.491), channel_id=1, source_target_pairs={{1,0},{2,1},{3,2},{4,3},{5,4},{6,5},{7,6},{8,7},{9,8},{10,9},{11,1... | collective-permute-start | bytes 6291464 | tf_op jit(solution)/shard_map/while/body/eval_jaxpr/ppermute | solution.py:13
  451.2 183.3 %collective-permute-start = (bf16[128,8192]{1,0:T(8,128)(2,1)}, bf16[128,8192]{1,0:T(8,128)(2,1)S(1)}, u32[]{:S(2)}, u32[]{:S(2)}) collective-permute-start(bf16[128,8192]{1,0:T(8,128)(2,1)} %get-tuple-element.491), channel_id=1, source_target_pairs={{1,0},{2,1},{3,2},{4,3},{5,4},{6,5},{7,6},{8,7},{9,8},{10,9},{11,1... | collective-permute-start | bytes 6291464 | tf_op jit(solution)/shard_map/while/body/eval_jaxpr/ppermute | solution.py:13
  634.5 9.0 %slice-start = ((s8[8388608]{0:T(1024)(128)(4,1)}), s8[4194304]{0:T(1024)(128)(4,1)S(1)}, s32[]{:S(2)}) async-start(s8[8388608]{0:T(1024)(128)(4,1)} %bitcast.45), calls=%async_computation | async-start | bytes 8388608 | tf_op jit(solution)/shard_map/while/body/eval_jaxpr/cond
  637.0 6.5 slice-start.1
  656.6 31.2 %collective-permute-start = (bf16[128,8192]{1,0:T(8,128)(2,1)}, bf16[128,8192]{1,0:T(8,128)(2,1)S(1)}, u32[]{:S(2)}, u32[]{:S(2)}) collective-permute-start(bf16[128,8192]{1,0:T(8,128)(2,1)} %get-tuple-element.491), channel_id=1, source_target_pairs={{1,0},{2,1},{3,2},{4,3},{5,4},{6,5},{7,6},{8,7},{9,8},{10,9},{11,1... | collective-permute-start | bytes 6291464 | tf_op jit(solution)/shard_map/while/body/eval_jaxpr/ppermute | solution.py:13
  687.8 9.0 %slice-start = ((s8[8388608]{0:T(1024)(128)(4,1)}), s8[4194304]{0:T(1024)(128)(4,1)S(1)}, s32[]{:S(2)}) async-start(s8[8388608]{0:T(1024)(128)(4,1)} %bitcast.45), calls=%async_computation | async-start | bytes 8388608 | tf_op jit(solution)/shard_map/while/body/eval_jaxpr/cond
  690.3 6.5 slice-start.1
  709.8 31.2 %collective-permute-start = (bf16[128,8192]{1,0:T(8,128)(2,1)}, bf16[128,8192]{1,0:T(8,128)(2,1)S(1)}, u32[]{:S(2)}, u32[]{:S(2)}) collective-permute-start(bf16[128,8192]{1,0:T(8,128)(2,1)} %get-tuple-element.491), channel_id=1, source_target_pairs={{1,0},{2,1},{3,2},{4,3},{5,4},{6,5},{7,6},{8,7},{9,8},{10,9},{11,1... | collective-permute-start | bytes 6291464 | tf_op jit(solution)/shard_map/while/body/eval_jaxpr/ppermute | solution.py:13
  741.0 9.0 %slice-start = ((s8[8388608]{0:T(1024)(128)(4,1)}), s8[4194304]{0:T(1024)(128)(4,1)S(1)}, s32[]{:S(2)}) async-start(s8[8388608]{0:T(1024)(128)(4,1)} %bitcast.45), calls=%async_computation | async-start | bytes 8388608 | tf_op jit(solution)/shard_map/while/body/eval_jaxpr/cond
  743.6 6.5 slice-start.1
  763.1 30.4 %collective-permute-start = (bf16[128,8192]{1,0:T(8,128)(2,1)}, bf16[128,8192]{1,0:T(8,128)(2,1)S(1)}, u32[]{:S(2)}, u32[]{:S(2)}) collective-permute-start(bf16[128,8192]{1,0:T(8,128)(2,1)} %get-tuple-element.491), channel_id=1, source_target_pairs={{1,0},{2,1},{3,2},{4,3},{5,4},{6,5},{7,6},{8,7},{9,8},{10,9},{11,1... | collective-permute-start | bytes 6291464 | tf_op jit(solution)/shard_map/while/body/eval_jaxpr/ppermute | solution.py:13
  793.5 9.0 %slice-start = ((s8[8388608]{0:T(1024)(128)(4,1)}), s8[4194304]{0:T(1024)(128)(4,1)S(1)}, s32[]{:S(2)}) async-start(s8[8388608]{0:T(1024)(128)(4,1)} %bitcast.45), calls=%async_computation | async-start | bytes 8388608 | tf_op jit(solution)/shard_map/while/body/eval_jaxpr/cond
  796.0 6.5 slice-start.1
  815.4 7.2 collective-permute-start
